TPU v7x, 32 devices: a whole 2x2x4 slice. The times are simulated.
32 devices in a mesh: fsdp: 8 (over y, x, core), shard: 4 (over z).
Axes of the slice: x: 2, y: 2, z: 4, core: 2. Of those that a mesh axis runs over, the one named last changes fastest.
Arguments:
- tokens: bfloat16 [4096, 1024], P(('fsdp', 'shard')), may hold values from -6 to 6
- cotangent: bfloat16 [4096, 1024], P(('fsdp', 'shard')), may hold values from -6 to 6
- starts: int32 [4096], P(('fsdp', 'shard')), may hold values from 0 to 127, as said below
- counts: int32 [32], P(('fsdp', 'shard')), may hold values from 64 to 128, as said below
- attn_gain: bfloat16 [4, 256], P('shard', 'fsdp'), may hold values from 0.5 to 1.5
- attn_shift: bfloat16 [4, 256], P('shard', 'fsdp'), may hold values from -1.75 to 1.75
- w_qkv: bfloat16 [1024, 3, 1024], P('fsdp', None, 'shard'), may hold values from -0.1875 to 0.1875
- query_bias: bfloat16 [4, 256], P('shard', 'fsdp'), may hold values from -1.75 to 1.75
- value_bias: bfloat16 [4, 256], P('shard', 'fsdp'), may hold values from -1.75 to 1.75
- w_proj: bfloat16 [1024, 1024], P('shard', 'fsdp'), may hold values from -0.75 to 0.75
- proj_bias: bfloat16 [4, 256], P('shard', 'fsdp'), may hold values from -1.75 to 1.75
- mlp_gain: bfloat16 [4, 256], P('shard', 'fsdp'), may hold values from 0.5 to 1.5
- mlp_shift: bfloat16 [4, 256], P('shard', 'fsdp'), may hold values from -1.75 to 1.75
- w_up: bfloat16 [1024, 4096], P('fsdp', 'shard'), may hold values from -0.1875 to 0.1875
- up_bias: bfloat16 [4, 1024], P('shard', 'fsdp'), may hold values from -1.75 to 1.75
- w_down: bfloat16 [4096, 1024], P('shard', 'fsdp'), may hold values from -0.375 to 0.375
- down_bias: bfloat16 [4, 256], P('shard', 'fsdp'), may hold values from -1.75 to 1.75
Outputs:
- block_out: bfloat16 [4096, 1024], P(('fsdp', 'shard'))
- grad_tokens: float32 [4096, 1024], P(('fsdp', 'shard'))
- grad_attn_gain: float32 [4, 256], P('shard', 'fsdp')
- grad_attn_shift: float32 [4, 256], P('shard', 'fsdp')
- grad_w_qkv: float32 [1024, 3, 1024], P('fsdp', None, 'shard')
- grad_query_bias: float32 [4, 256], P('shard', 'fsdp')
- grad_value_bias: float32 [4, 256], P('shard', 'fsdp')
- grad_w_proj: float32 [1024, 1024], P('shard', 'fsdp')
- grad_proj_bias: float32 [4, 256], P('shard', 'fsdp')
- grad_mlp_gain: float32 [4, 256], P('shard', 'fsdp')
- grad_mlp_shift: float32 [4, 256], P('shard', 'fsdp')
- grad_w_up: float32 [1024, 4096], P('fsdp', 'shard')
- grad_up_bias: float32 [4, 1024], P('shard', 'fsdp')
- grad_w_down: float32 [4096, 1024], P('shard', 'fsdp')
- grad_down_bias: float32 [4, 256], P('shard', 'fsdp')
Inputs may be any that keep to these rules, and one draw needn't show every extreme that they name: starts[s] is the index, inside the block of 128 slots that holds slot s, of the first slot of s's sequence; a sequence's slots are consecutive in one block and never cross blocks; slots at or past the block's live count start themselves; in every draw some block holds one sequence over all 128 slots. The live slots are the first counts[b] of block b; some block is full in every draw.
All inputs are finite; a program needn't handle non-finite values.
Results may differ from a plain program's by a relative error of at most 0.012.
Values may be sent and summed in bfloat16 or wider, within the bound.
No kernel may reach another device: no remote copies, remote signals or barrier semaphores. Data moves between devices by JAX's collectives and lax.ppermute only.
A program may use at most 128 MiB of HBM per device.

v0:
```python
import jax
import jax.numpy as jnp
from jax import lax
from jax.sharding import PartitionSpec as P

HEAD_DIM = 64
NORM_EPS = 1e-05
NEG_FILL = -1e30


def layer_norm(inputs, norm_gain, norm_shift):
    center = inputs - jnp.mean(inputs, axis=-1, keepdims=True)
    variance = jnp.mean(center * center, axis=-1, keepdims=True)
    return center * lax.rsqrt(variance + NORM_EPS) * norm_gain + norm_shift


def gelu_tanh(values):
    return jax.nn.gelu(values, approximate=True)


def split_heads(qkv_full, quarter, slot_count):
    row_count = qkv_full.shape[0]
    grid = (row_count // slot_count, slot_count, quarter // HEAD_DIM, HEAD_DIM)
    query_part = qkv_full[:, :quarter].reshape(grid)
    key_part = qkv_full[:, quarter : 2 * quarter].reshape(grid)
    value_part = qkv_full[:, 2 * quarter :].reshape(grid)
    return (query_part, key_part, value_part)


def score_blocks(query_part, key_part, starts_grid):
    scores = jnp.einsum("bqhd,bkhd->bhqk", query_part, key_part, preferred_element_type=jnp.float32)
    scores = scores * HEAD_DIM ** (-0.5)
    positions = jnp.arange(scores.shape[2], dtype=jnp.int32)
    visible = (positions[None, None, :] >= starts_grid[:, :, None]) & (
        positions[None, None, :] <= positions[None, :, None]
    )
    return jnp.where(visible[:, None], scores, NEG_FILL)


def collect(params):
    over = (
        lax.all_gather(params[0], "fsdp", axis=1, tiled=True),
        lax.all_gather(params[1], "fsdp", axis=1, tiled=True),
        lax.all_gather(params[2], "fsdp", axis=0, tiled=True),
        lax.all_gather(params[3], "fsdp", axis=1, tiled=True),
        lax.all_gather(params[4], "fsdp", axis=1, tiled=True),
        lax.all_gather(params[5], "fsdp", axis=1, tiled=True),
        lax.all_gather(params[6], "fsdp", axis=1, tiled=True),
        lax.all_gather(params[7], "fsdp", axis=1, tiled=True),
        lax.all_gather(params[8], "fsdp", axis=1, tiled=True),
        lax.all_gather(params[9], "fsdp", axis=0, tiled=True),
        lax.all_gather(params[10], "fsdp", axis=1, tiled=True),
        lax.all_gather(params[11], "fsdp", axis=1, tiled=True),
        lax.all_gather(params[12], "fsdp", axis=1, tiled=True),
    )
    vectors = (
        lax.all_gather(over[0], "shard", axis=0, tiled=True),
        lax.all_gather(over[1], "shard", axis=0, tiled=True),
        lax.all_gather(over[6], "shard", axis=0, tiled=True),
        lax.all_gather(over[7], "shard", axis=0, tiled=True),
        lax.all_gather(over[8], "shard", axis=0, tiled=True),
        lax.all_gather(over[12], "shard", axis=0, tiled=True),
    )
    full = (
        vectors[0].reshape(-1),
        vectors[1].reshape(-1),
        over[2],
        over[3].reshape(-1),
        over[4].reshape(-1),
        over[5],
        vectors[2].reshape(-1),
        vectors[3].reshape(-1),
        vectors[4].reshape(-1),
        over[9],
        over[10].reshape(-1),
        over[11],
        vectors[5].reshape(-1),
    )
    return full


def spread(grads, shard_count):
    (
        g_attn_gain,
        g_attn_shift,
        g_qkv,
        g_query_bias,
        g_value_bias,
        g_proj,
        g_proj_bias,
        g_mlp_gain,
        g_mlp_shift,
        g_up,
        g_up_bias,
        g_down,
        g_down_bias,
    ) = grads
    summed = (
        lax.psum_scatter(
            g_attn_gain.reshape(shard_count, -1), "shard", scatter_dimension=0, tiled=True
        ),
        lax.psum_scatter(
            g_attn_shift.reshape(shard_count, -1), "shard", scatter_dimension=0, tiled=True
        ),
        lax.psum_scatter(
            g_proj_bias.reshape(shard_count, -1), "shard", scatter_dimension=0, tiled=True
        ),
        lax.psum_scatter(
            g_mlp_gain.reshape(shard_count, -1), "shard", scatter_dimension=0, tiled=True
        ),
        lax.psum_scatter(
            g_mlp_shift.reshape(shard_count, -1), "shard", scatter_dimension=0, tiled=True
        ),
        lax.psum_scatter(
            g_down_bias.reshape(shard_count, -1), "shard", scatter_dimension=0, tiled=True
        ),
    )
    pieces = (
        summed[0],
        summed[1],
        g_qkv,
        g_query_bias.reshape(1, -1),
        g_value_bias.reshape(1, -1),
        g_proj,
        summed[2],
        summed[3],
        summed[4],
        g_up,
        g_up_bias.reshape(1, -1),
        g_down,
        summed[5],
    )
    owned = (
        lax.psum_scatter(pieces[0], "fsdp", scatter_dimension=1, tiled=True),
        lax.psum_scatter(pieces[1], "fsdp", scatter_dimension=1, tiled=True),
        lax.psum_scatter(pieces[2], "fsdp", scatter_dimension=0, tiled=True),
        lax.psum_scatter(pieces[3], "fsdp", scatter_dimension=1, tiled=True),
        lax.psum_scatter(pieces[4], "fsdp", scatter_dimension=1, tiled=True),
        lax.psum_scatter(pieces[5], "fsdp", scatter_dimension=1, tiled=True),
        lax.psum_scatter(pieces[6], "fsdp", scatter_dimension=1, tiled=True),
        lax.psum_scatter(pieces[7], "fsdp", scatter_dimension=1, tiled=True),
        lax.psum_scatter(pieces[8], "fsdp", scatter_dimension=1, tiled=True),
        lax.psum_scatter(pieces[9], "fsdp", scatter_dimension=0, tiled=True),
        lax.psum_scatter(pieces[10], "fsdp", scatter_dimension=1, tiled=True),
        lax.psum_scatter(pieces[11], "fsdp", scatter_dimension=1, tiled=True),
        lax.psum_scatter(pieces[12], "fsdp", scatter_dimension=1, tiled=True),
    )
    return owned


def forward_pass(full, tokens, starts, live):
    (
        attn_gain,
        attn_shift,
        w_qkv,
        query_bias,
        value_bias,
        w_proj,
        proj_bias,
        mlp_gain,
        mlp_shift,
        w_up,
        up_bias,
        w_down,
        down_bias,
    ) = full
    slot_count = tokens.shape[0]
    width = tokens.shape[1]
    tokens_wide = tokens.astype(jnp.float32)
    normed_attn = layer_norm(
        tokens_wide, attn_gain.astype(jnp.float32), attn_shift.astype(jnp.float32)
    )
    act_attn = normed_attn.astype(jnp.bfloat16)
    act_rows, start_rows = (
        lax.all_gather(act_attn, "shard", axis=0, tiled=True),
        lax.all_gather(starts, "shard", axis=0, tiled=True),
    )
    quarter = w_qkv.shape[2]
    row_count = act_rows.shape[0]
    qkv_bias = jnp.concatenate([query_bias, jnp.zeros_like(query_bias), value_bias]).astype(
        jnp.float32
    )
    qkv_full = (
        jnp.dot(act_rows, w_qkv.reshape(width, 3 * quarter), preferred_element_type=jnp.float32)
        + qkv_bias
    ).astype(jnp.bfloat16)
    query_part, key_part, value_part = split_heads(qkv_full, quarter, slot_count)
    starts_grid = start_rows.reshape(row_count // slot_count, slot_count)
    scores = score_blocks(query_part, key_part, starts_grid)
    row_max = jnp.max(scores, axis=-1, keepdims=True)
    log_total = row_max + jnp.log(jnp.sum(jnp.exp(scores - row_max), axis=-1, keepdims=True))
    probs_low = jnp.exp(scores - log_total).astype(jnp.bfloat16)
    mixed = jnp.einsum("bhqk,bkhd->bqhd", probs_low, value_part, preferred_element_type=jnp.float32)
    mixed = mixed.reshape(row_count, quarter).astype(jnp.bfloat16)
    attn_term = lax.psum_scatter(
        jnp.dot(mixed, w_proj, preferred_element_type=jnp.float32),
        "shard",
        scatter_dimension=0,
        tiled=True,
    )
    hidden_one = tokens_wide + attn_term + proj_bias.astype(jnp.float32)
    normed_mlp = layer_norm(hidden_one, mlp_gain.astype(jnp.float32), mlp_shift.astype(jnp.float32))
    act_mlp = normed_mlp.astype(jnp.bfloat16)
    mlp_inputs = lax.all_gather(act_mlp, "shard", axis=0, tiled=True)
    pre_act = jnp.dot(mlp_inputs, w_up, preferred_element_type=jnp.float32) + up_bias.astype(
        jnp.float32
    )
    act_up = gelu_tanh(pre_act).astype(jnp.bfloat16)
    mlp_term = lax.psum_scatter(
        jnp.dot(act_up, w_down, preferred_element_type=jnp.float32),
        "shard",
        scatter_dimension=0,
        tiled=True,
    )
    block_out = (hidden_one + mlp_term + down_bias.astype(jnp.float32)) * live
    saved = (
        act_rows,
        starts_grid,
        qkv_full,
        log_total,
        mixed,
        hidden_one,
        mlp_inputs,
        pre_act,
        act_up,
    )
    return (block_out.astype(jnp.bfloat16), saved)


def backward_pass(full, saved, tokens, cotangent, live):
    (
        attn_gain,
        attn_shift,
        w_qkv,
        query_bias,
        value_bias,
        w_proj,
        proj_bias,
        mlp_gain,
        mlp_shift,
        w_up,
        up_bias,
        w_down,
        down_bias,
    ) = full
    act_rows, starts_grid, qkv_full, log_total, mixed, hidden_one, mlp_inputs, pre_act, act_up = (
        saved
    )
    slot_count = tokens.shape[0]
    width = tokens.shape[1]
    quarter = w_qkv.shape[2]
    row_count = act_rows.shape[0]
    tokens_wide = tokens.astype(jnp.float32)
    grad_out = cotangent.astype(jnp.float32) * live
    grad_low = grad_out.astype(jnp.bfloat16)
    grad_low_rows = lax.all_gather(grad_low, "shard", axis=0, tiled=True)
    g_down = jnp.dot(act_up.T, grad_low_rows, preferred_element_type=jnp.float32)
    g_down_bias = jnp.sum(grad_out, axis=0)
    grad_act = jnp.dot(grad_low_rows, w_down.T, preferred_element_type=jnp.float32)
    gelu_value, gelu_back = jax.vjp(gelu_tanh, pre_act)
    (grad_pre,) = gelu_back(grad_act)
    grad_pre_low = grad_pre.astype(jnp.bfloat16)
    g_up = jnp.dot(mlp_inputs.T, grad_pre_low, preferred_element_type=jnp.float32)
    g_up_bias = jnp.sum(grad_pre, axis=0)
    grad_normed = lax.psum_scatter(
        jnp.dot(grad_pre_low, w_up.T, preferred_element_type=jnp.float32),
        "shard",
        scatter_dimension=0,
        tiled=True,
    )
    norm_value, norm_back = jax.vjp(
        layer_norm, hidden_one, mlp_gain.astype(jnp.float32), mlp_shift.astype(jnp.float32)
    )
    grad_hidden_part, g_mlp_gain, g_mlp_shift = norm_back(grad_normed)
    grad_hidden = grad_out + grad_hidden_part
    grad_hidden_low = grad_hidden.astype(jnp.bfloat16)
    hidden_rows = lax.all_gather(grad_hidden_low, "shard", axis=0, tiled=True)
    g_proj = jnp.dot(mixed.T, hidden_rows, preferred_element_type=jnp.float32)
    g_proj_bias = jnp.sum(grad_hidden, axis=0)
    grad_mixed = jnp.dot(hidden_rows, w_proj.T, preferred_element_type=jnp.float32).astype(
        jnp.bfloat16
    )
    grad_mixed = grad_mixed.reshape(
        row_count // slot_count, slot_count, quarter // HEAD_DIM, HEAD_DIM
    )
    query_part, key_part, value_part = split_heads(qkv_full, quarter, slot_count)
    scores = score_blocks(query_part, key_part, starts_grid)
    attn_probs = jnp.exp(scores - log_total)
    probs_low = attn_probs.astype(jnp.bfloat16)
    grad_probs = jnp.einsum(
        "bqhd,bkhd->bhqk", grad_mixed, value_part, preferred_element_type=jnp.float32
    )
    grad_value = jnp.einsum(
        "bhqk,bqhd->bkhd", probs_low, grad_mixed, preferred_element_type=jnp.float32
    )
    row_dot = jnp.sum(attn_probs * grad_probs, axis=-1, keepdims=True)
    grad_scores = (attn_probs * (grad_probs - row_dot) * HEAD_DIM ** (-0.5)).astype(jnp.bfloat16)
    grad_query = jnp.einsum(
        "bhqk,bkhd->bqhd", grad_scores, key_part, preferred_element_type=jnp.float32
    )
    grad_key = jnp.einsum(
        "bhqk,bqhd->bkhd", grad_scores, query_part, preferred_element_type=jnp.float32
    )
    grad_query = grad_query.reshape(row_count, quarter)
    grad_key = grad_key.reshape(row_count, quarter)
    grad_value = grad_value.reshape(row_count, quarter)
    g_query_bias = jnp.sum(grad_query, axis=0)
    g_value_bias = jnp.sum(grad_value, axis=0)
    grad_qkv_low = jnp.concatenate([grad_query, grad_key, grad_value], axis=1).astype(jnp.bfloat16)
    g_qkv = jnp.dot(act_rows.T, grad_qkv_low, preferred_element_type=jnp.float32).reshape(
        width, 3, quarter
    )
    qkv_matrix = w_qkv.reshape(width, 3 * quarter)
    grad_normed_attn = lax.psum_scatter(
        jnp.dot(grad_qkv_low, qkv_matrix.T, preferred_element_type=jnp.float32),
        "shard",
        scatter_dimension=0,
        tiled=True,
    )
    first_value, first_back = jax.vjp(
        layer_norm, tokens_wide, attn_gain.astype(jnp.float32), attn_shift.astype(jnp.float32)
    )
    grad_in_part, g_attn_gain, g_attn_shift = first_back(grad_normed_attn)
    grad_in = grad_hidden + grad_in_part
    grads = (
        g_attn_gain,
        g_attn_shift,
        g_qkv,
        g_query_bias,
        g_value_bias,
        g_proj,
        g_proj_bias,
        g_mlp_gain,
        g_mlp_shift,
        g_up,
        g_up_bias,
        g_down,
        g_down_bias,
    )
    return (grad_in, grads)


def on_device(
    tokens,
    cotangent,
    starts,
    counts,
    attn_gain,
    attn_shift,
    w_qkv,
    query_bias,
    value_bias,
    w_proj,
    proj_bias,
    mlp_gain,
    mlp_shift,
    w_up,
    up_bias,
    w_down,
    down_bias,
):
    shard_count = lax.axis_size("shard")
    params = (
        attn_gain,
        attn_shift,
        w_qkv,
        query_bias,
        value_bias,
        w_proj,
        proj_bias,
        mlp_gain,
        mlp_shift,
        w_up,
        up_bias,
        w_down,
        down_bias,
    )
    full_forward = collect(params)
    live = (jnp.arange(tokens.shape[0], dtype=jnp.int32) < counts[0]).astype(jnp.float32)[:, None]
    output_low, saved = forward_pass(full_forward, tokens, starts, live)
    full_backward = collect(params)
    grad_in, grads = backward_pass(full_backward, saved, tokens, cotangent, live)
    owned = spread(grads, shard_count)
    return (
        output_low,
        grad_in,
        owned[0],
        owned[1],
        owned[2],
        owned[3],
        owned[4],
        owned[5],
        owned[6],
        owned[7],
        owned[8],
        owned[9],
        owned[10],
        owned[11],
        owned[12],
    )


def solution(mesh):
    in_specs = (
        P(("fsdp", "shard"), None),
        P(("fsdp", "shard"), None),
        P(("fsdp", "shard")),
        P(("fsdp", "shard")),
        P("shard", "fsdp"),
        P("shard", "fsdp"),
        P("fsdp", None, "shard"),
        P("shard", "fsdp"),
        P("shard", "fsdp"),
        P("shard", "fsdp"),
        P("shard", "fsdp"),
        P("shard", "fsdp"),
        P("shard", "fsdp"),
        P("fsdp", "shard"),
        P("shard", "fsdp"),
        P("shard", "fsdp"),
        P("shard", "fsdp"),
    )
    out_specs = (
        P(("fsdp", "shard"), None),
        P(("fsdp", "shard"), None),
        P("shard", "fsdp"),
        P("shard", "fsdp"),
        P("fsdp", None, "shard"),
        P("shard", "fsdp"),
        P("shard", "fsdp"),
        P("shard", "fsdp"),
        P("shard", "fsdp"),
        P("shard", "fsdp"),
        P("shard", "fsdp"),
        P("fsdp", "shard"),
        P("shard", "fsdp"),
        P("shard", "fsdp"),
        P("shard", "fsdp"),
    )
    return jax.shard_map(
        on_device, mesh=mesh, in_specs=in_specs, out_specs=out_specs, check_vma=False
    )
```

profile of v0, /device:TPU:0, one launch (start us, length us, event | category | flops | bytes accessed | tf_op | source)
XLA Modules:
  0.0 999.4 jit_solution(1785968189932253058)
XLA Ops:
  15.9 15.1 %all-reduce.15 = (bf16[256]{0:T(256)(128)(2,1)S(1)}, bf16[256]{0:T(256)(128)(2,1)S(1)}, bf16[256]{0:T(256)(128)(2,1)S(1)}, bf16[256]{0:T(256)(128)(2,1)S(1)}, bf...) all-reduce(bf16[256]{0:T(256)(128)(2,1)S(1)} %dynamic-update-slice., ...), channel_id=1, replica_groups=mesh['fsdp'=8,'shard'=4] {'fsdp'}, use_global_device_ids=true, to_apply=%add.1 | all-reduce | flops 2048 | bytes 8192
  31.1 11.2 %all-gather = bf16[4,1,256]{2,1,0:T(2,128)(2,1)S(1)} all-gather(bf16[1,1,256]{2,1,0:T(2,128)(2,1)S(1)} %reshape.313), channel_id=1, replica_groups=mesh['fsdp'=8,'shard'=4] {'shard'}, dimensions={0}, use_global_device_ids=true | all-gather | bytes 2560 | tf_op jit(solution)/shard_map/all_gather | solution.py:57
  55.9 9.7 all-gather.2
  65.6 9.0 all_gather.89
  79.9 27.8 %all-gather.17.cloned.1.call-done = bf16[1024,3,256]{0,2,1:T(8,128)(2,1)} async-done(((bf16[128,3,256]{0,2,1:T(8,128)(2,1)}), bf16[1024,3,256]{0,2,1:T(8,128)(2,1)}) %all-gather.17.cloned.1.call-update) | async-done | bytes 1572880 | tf_op jit(solution)/shard_map/all_gather | solution.py:44
  115.7 10.9 %all-gather.3 = bf16[4,1,256]{2,1,0:T(2,128)(2,1)S(1)} all-gather(bf16[1,1,256]{2,1,0:T(2,128)(2,1)S(1)} %reshape.319), channel_id=1, replica_groups=mesh['fsdp'=8,'shard'=4] {'shard'}, dimensions={0}, use_global_device_ids=true | all-gather | bytes 2560 | tf_op jit(solution)/shard_map/all_gather | solution.py:59
  126.6 7.8 all-gather.4
  134.4 10.3 %all-gather.5 = bf16[4,1,256]{2,1,0:T(2,128)(2,1)S(1)} all-gather(bf16[1,1,256]{2,1,0:T(2,128)(2,1)S(1)} %reshape.323), channel_id=1, replica_groups=mesh['fsdp'=8,'shard'=4] {'shard'}, dimensions={0}, use_global_device_ids=true | all-gather | bytes 2560 | tf_op jit(solution)/shard_map/all_gather | solution.py:61
  144.8 14.4 %reduce-scatter.36.cloned.1.call-done = f32[128,1024]{1,0:T(8,128)} async-done(((f32[512,1024]{1,0:T(8,128)}), f32[128,1024]{1,0:T(8,128)}) %reduce-scatter.36.cloned.1.call-update) | async-done | bytes 524304 | tf_op jit(solution)/shard_map/reduce_scatter | solution.py:195
  163.9 8.9 all_gather.98
  172.8 15.5 %all-gather.21.cloned.1.call-done = bf16[1024,1024]{1,0:T(8,128)(2,1)} async-done(((bf16[128,1024]{1,0:T(8,128)(2,1)}), bf16[1024,1024]{1,0:T(8,128)(2,1)}) %all-gather.21.cloned.1.call-update) | async-done | bytes 2097168 | tf_op jit(solution)/shard_map/all_gather | solution.py:51
  188.3 30.0 %all-gather.19.cloned.1.call-done = bf16[512,1024]{1,0:T(8,128)(2,1)} async-done(((bf16[128,1024]{1,0:T(8,128)(2,1)}), bf16[512,1024]{1,0:T(8,128)(2,1)}) %all-gather.19.cloned.1.call-update) | async-done | bytes 1048592 | tf_op jit(solution)/shard_map/all_gather | solution.py:204
  222.8 25.0 %all-gather.25.cloned.1.call-done = bf16[512,1024]{1,0:T(8,128)(2,1)} async-done(((bf16[128,1024]{1,0:T(8,128)(2,1)}), bf16[512,1024]{1,0:T(8,128)(2,1)}) %all-gather.25.cloned.1.call-update) | async-done | bytes 1048592 | tf_op jit(solution)/shard_map/all_gather | solution.py:256
  247.9 29.8 %all-gather.23.cloned.1.call-done = bf16[1024,1024]{1,0:T(8,128)(2,1)} async-done(((bf16[1024,128]{1,0:T(8,128)(2,1)}), bf16[1024,1024]{1,0:T(8,128)(2,1)}) %all-gather.23.cloned.1.call-update) | async-done | bytes 2097168 | tf_op jit(solution)/shard_map/all_gather | solution.py:53
  291.7 11.2 %all-gather.6 = bf16[4,1,256]{2,1,0:T(2,128)(2,1)S(1)} all-gather(bf16[1,1,256]{2,1,0:T(2,128)(2,1)S(1)} %reshape.325), channel_id=1, replica_groups=mesh['fsdp'=8,'shard'=4] {'shard'}, dimensions={0}, use_global_device_ids=true | all-gather | bytes 2560 | tf_op jit(solution)/shard_map/all_gather | solution.py:62
  302.8 27.7 %reduce-scatter.40.cloned.1.call-done = f32[128,1024]{1,0:T(8,128)} async-done(((f32[512,1024]{1,0:T(8,128)}), f32[128,1024]{1,0:T(8,128)}) %reduce-scatter.40.cloned.1.call-update) | async-done | bytes 524304 | tf_op jit(solution)/shard_map/reduce_scatter | solution.py:265
  331.9 44.2 %reduce-scatter.38.cloned.1.call-done = f32[128,1024]{1,0:T(8,128)} async-done(((f32[512,1024]{1,0:T(8,128)}), f32[128,1024]{1,0:T(8,128)}) %reduce-scatter.38.cloned.1.call-update) | async-done | bytes 524304 | tf_op jit(solution)/shard_map/reduce_scatter | solution.py:209
  379.1 27.4 %all-gather.27.cloned.1.call-done = bf16[512,1024]{1,0:T(8,128)(2,1)} async-done(((bf16[128,1024]{1,0:T(8,128)(2,1)}), bf16[512,1024]{1,0:T(8,128)(2,1)}) %all-gather.27.cloned.1.call-update) | async-done | bytes 1048592 | tf_op jit(solution)/shard_map/all_gather | solution.py:277
  423.1 40.0 %reduce-scatter.42.cloned.1.call-done = f32[128,1024]{1,0:T(8,128)} async-done(((f32[512,1024]{1,0:T(8,128)}), f32[128,1024]{1,0:T(8,128)}) %reduce-scatter.42.cloned.1.call-update) | async-done | bytes 524304 | tf_op jit(solution)/shard_map/reduce_scatter | solution.py:314
  468.1 17.1 %all-reduce.14 = (f32[4,256]{1,0:T(4,128)S(1)}, f32[4,256]{1,0:T(4,128)S(1)}, f32[4,256]{1,0:T(4,128)S(1)}, f32[4,256]{1,0:T(4,128)S(1)}, f32[4,256]{1,0:T(4,128)S(1)}, /*index=5*/f32[4,256]{1,0:T(4,128)S(1)}) all-reduce(f32[4,256]{1,0:T(4,128)S(1)} %reshape.272, ...), channel_id=6, replica_groups=mesh['fsdp'=8,'shard'=4] {'shard'}, use_global_device_ids=true, to_apply=%region_16.17.clone | all-reduce | flops 6144 | bytes 49152
  511.4 24.8 %reduce-scatter.58.cloned.1.call-done = f32[32,1]{1,0:T(8,128)} async-done(((f32[256,1]{1,0:T(8,128)}), f32[32,1]{1,0:T(8,128)}) %reduce-scatter.58.cloned.1.call-update) | async-done | bytes 144
  537.5 35.0 %reduce-scatter.56.cloned.1.call-done = f32[32,1]{1,0:T(8,128)} async-done(((f32[256,1]{1,0:T(8,128)}), f32[32,1]{1,0:T(8,128)}) %reduce-scatter.56.cloned.1.call-update) | async-done | bytes 144
  573.8 35.2 %reduce-scatter.64.cloned.1.call-done = f32[32,1]{1,0:T(8,128)} async-done(((f32[256,1]{1,0:T(8,128)}), f32[32,1]{1,0:T(8,128)}) %reduce-scatter.64.cloned.1.call-update) | async-done | bytes 144
  610.3 35.0 %reduce-scatter.68.cloned.1.call-done = f32[32,1]{1,0:T(8,128)} async-done(((f32[256,1]{1,0:T(8,128)}), f32[32,1]{1,0:T(8,128)}) %reduce-scatter.68.cloned.1.call-update) | async-done | bytes 144
  646.6 35.2 %reduce-scatter.60.cloned.1.call-done = f32[32,1]{1,0:T(8,128)} async-done(((f32[256,1]{1,0:T(8,128)}), f32[32,1]{1,0:T(8,128)}) %reduce-scatter.60.cloned.1.call-update) | async-done | bytes 144
  683.1 35.0 %reduce-scatter.62.cloned.1.call-done = f32[32,1]{1,0:T(8,128)} async-done(((f32[256,1]{1,0:T(8,128)}), f32[32,1]{1,0:T(8,128)}) %reduce-scatter.62.cloned.1.call-update) | async-done | bytes 144
  719.4 35.3 %reduce-scatter.52.cloned.1.call-done = f32[32,1]{1,0:T(8,128)} async-done(((f32[256,1]{1,0:T(8,128)}), f32[32,1]{1,0:T(8,128)}) %reduce-scatter.52.cloned.1.call-update) | async-done | bytes 144
  756.0 35.0 %reduce-scatter.54.cloned.1.call-done = f32[32,1]{1,0:T(8,128)} async-done(((f32[256,1]{1,0:T(8,128)}), f32[32,1]{1,0:T(8,128)}) %reduce-scatter.54.cloned.1.call-update) | async-done | bytes 144
  792.3 54.4 %reduce-scatter.48.cloned.1.call-done = f32[128,1024]{1,0:T(8,128)} async-done(((f32[1024,1024]{1,0:T(8,128)}), f32[128,1024]{1,0:T(8,128)}) %reduce-scatter.48.cloned.1.call-update) | async-done | bytes 524304 | tf_op jit(solution)/shard_map/reduce_scatter | solution.py:143
  846.6 55.3 %reduce-scatter.50.cloned.1.call-done = f32[1024,128]{1,0:T(8,128)} async-done(((f32[1024,1024]{1,0:T(8,128)}), f32[1024,128]{1,0:T(8,128)}) %reduce-scatter.50.cloned.1.call-update) | async-done | bytes 524304 | tf_op jit(solution)/shard_map/reduce_scatter | solution.py:145
  901.9 40.2 %reduce-scatter.46.cloned.1.call-done = f32[256,128]{1,0:T(8,128)} async-done(((f32[256,1024]{1,0:T(8,128)}), f32[256,128]{1,0:T(8,128)}) %reduce-scatter.46.cloned.1.call-update) | async-done | bytes 131088 | tf_op jit(solution)/shard_map/reduce_scatter | solution.py:139
  942.1 50.5 %reduce-scatter.44.cloned.1.call-done = f32[128,3,256]{2,0,1:T(8,128)} async-done(((f32[1024,3,256]{2,0,1:T(8,128)}), f32[128,3,256]{2,0,1:T(8,128)}) %reduce-scatter.44.cloned.1.call-update) | async-done | bytes 393232 | tf_op jit(solution)/shard_map/reduce_scatter | solution.py:136
  (211 shorter events, 119.4 us)
Async XLA Ops:
  7.2 58.4 %copy-start.12 = (bf16[256,128]{1,0:T(8,128)(2,1)S(1)}, bf16[256,128]{1,0:T(8,128)(2,1)}, u32[]{:S(2)}) copy-start(bf16[256,128]{1,0:T(8,128)(2,1)} %param.26) | copy-start | bytes 196612
  7.2 72.7 %all-gather.15.cloned.1.call-start = ((), (), s32[]{:S(2)}) async-start(), calls=%async_computation.17 | async-start | bytes 1310720 | tf_op jit(solution)/shard_map/all_gather | solution.py:175
  54.0 53.7 %all-gather.17.cloned.1.call-start = ((), (), s32[]{:S(2)}) async-start(), calls=%async_computation.18 | async-start | bytes 1769472 | tf_op jit(solution)/shard_map/all_gather | solution.py:44
  55.8 103.4 %reduce-scatter.36.cloned.1.call-start = ((), (), s32[]{:S(2)}) async-start(), calls=%async_computation.19 | async-start | bytes 2621440 | tf_op jit(solution)/shard_map/reduce_scatter | solution.py:195
  74.6 38.6 %copy-start.3 = (bf16[256,1024]{1,0:T(8,128)(2,1)}, bf16[256,1024]{1,0:T(8,128)(2,1)S(1)}, u32[]{:S(2)}) copy-start(bf16[256,1024]{1,0:T(8,128)(2,1)S(1)} %all_gather.89) | copy-start | bytes 1572868
  113.2 46.0 %copy-start = (bf16[128,1024]{1,0:T(8,128)(2,1)S(1)}, bf16[128,1024]{1,0:T(8,128)(2,1)}, u32[]{:S(2)}) copy-start(bf16[128,1024]{1,0:T(8,128)(2,1)} %param.17) | copy-start | bytes 786436
  115.0 47.2 %copy-start.2 = (bf16[128,1024]{1,0:T(8,128)(2,1)S(1)}, bf16[128,1024]{1,0:T(8,128)(2,1)}, u32[]{:S(2)}) copy-start(bf16[128,1024]{1,0:T(8,128)(2,1)} %param.18) | copy-start | bytes 786436
  115.0 48.8 %copy-start.13 = (bf16[1,128]{1,0:T(2,128)(2,1)S(1)}, bf16[1,128]{1,0:T(2,128)(2,1)}, u32[]{:S(2)}) copy-start(bf16[1,128]{1,0:T(2,128)(2,1)} %param.31) | copy-start | bytes 772
  115.0 73.3 %all-gather.21.cloned.1.call-start = ((), (), s32[]{:S(2)}) async-start(), calls=%async_computation.21 | async-start | bytes 2359296 | tf_op jit(solution)/shard_map/all_gather | solution.py:51
  115.6 102.7 %all-gather.19.cloned.1.call-start = ((), (), s32[]{:S(2)}) async-start(), calls=%async_computation.20 | async-start | bytes 1310720 | tf_op jit(solution)/shard_map/all_gather | solution.py:204
  161.5 86.4 %all-gather.25.cloned.1.call-start = ((), (), s32[]{:S(2)}) async-start(), calls=%async_computation.24 | async-start | bytes 1310720 | tf_op jit(solution)/shard_map/all_gather | solution.py:256
  163.1 114.6 %all-gather.23.cloned.1.call-start = ((), (), s32[]{:S(2)}) async-start(), calls=%async_computation.22 | async-start | bytes 2359296 | tf_op jit(solution)/shard_map/all_gather | solution.py:53
  163.8 166.7 %reduce-scatter.40.cloned.1.call-start = ((), (), s32[]{:S(2)}) async-start(), calls=%async_computation.25 | async-start | bytes 2621440 | tf_op jit(solution)/shard_map/reduce_scatter | solution.py:265
  277.6 6.2 copy-start.14
  286.5 89.6 %reduce-scatter.38.cloned.1.call-start = ((), (), s32[]{:S(2)}) async-start(), calls=%async_computation.23 | async-start | bytes 2621440 | tf_op jit(solution)/shard_map/reduce_scatter | solution.py:209
  291.6 114.9 %all-gather.27.cloned.1.call-start = ((), (), s32[]{:S(2)}) async-start(), calls=%async_computation.26 | async-start | bytes 1310720 | tf_op jit(solution)/shard_map/all_gather | solution.py:277
  379.1 84.0 %reduce-scatter.42.cloned.1.call-start = ((), (), s32[]{:S(2)}) async-start(), calls=%async_computation.27 | async-start | bytes 2621440 | tf_op jit(solution)/shard_map/reduce_scatter | solution.py:314
  411.4 4.4 copy-start.10
  419.6 90.4 %reduce-scatter.66.cloned.1.call-start = ((), (), s32[]{:S(2)}) async-start(), calls=%async_computation.39 | async-start | bytes 589824
  420.7 115.5 %reduce-scatter.58.cloned.1.call-start = ((), (), s32[]{:S(2)}) async-start(), calls=%async_computation.35 | async-start | bytes 147456
  421.6 150.9 %reduce-scatter.56.cloned.1.call-start = ((), (), s32[]{:S(2)}) async-start(), calls=%async_computation.34 | async-start | bytes 147456
  423.1 186.0 %reduce-scatter.64.cloned.1.call-start = ((), (), s32[]{:S(2)}) async-start(), calls=%async_computation.38 | async-start | bytes 147456
  465.8 26.6 %copy-start.4 = (bf16[512,1024]{1,0:T(8,128)(2,1)S(1)}, bf16[512,1024]{1,0:T(8,128)(2,1)}, u32[]{:S(2)}) copy-start(bf16[512,1024]{1,0:T(8,128)(2,1)} %all-gather.19.cloned.1.call-done) | copy-start | bytes 3145732
  486.7 158.6 %reduce-scatter.68.cloned.1.call-start = ((), (), s32[]{:S(2)}) async-start(), calls=%async_computation.40 | async-start | bytes 147456
  487.5 194.2 %reduce-scatter.60.cloned.1.call-start = ((), (), s32[]{:S(2)}) async-start(), calls=%async_computation.36 | async-start | bytes 147456
  489.1 229.0 %reduce-scatter.62.cloned.1.call-start = ((), (), s32[]{:S(2)}) async-start(), calls=%async_computation.37 | async-start | bytes 147456
  489.9 264.8 %reduce-scatter.52.cloned.1.call-start = ((), (), s32[]{:S(2)}) async-start(), calls=%async_computation.32 | async-start | bytes 147456
  491.5 299.5 %reduce-scatter.54.cloned.1.call-start = ((), (), s32[]{:S(2)}) async-start(), calls=%async_computation.33 | async-start | bytes 147456
  492.3 354.3 %reduce-scatter.48.cloned.1.call-start = ((), (), s32[]{:S(2)}) async-start(), calls=%async_computation.30 | async-start | bytes 4718592 | tf_op jit(solution)/shard_map/reduce_scatter | solution.py:143
  496.9 405.0 %reduce-scatter.50.cloned.1.call-start = ((), (), s32[]{:S(2)}) async-start(), calls=%async_computation.31 | async-start | bytes 4718592 | tf_op jit(solution)/shard_map/reduce_scatter | solution.py:145
  502.4 439.7 %reduce-scatter.46.cloned.1.call-start = ((), (), s32[]{:S(2)}) async-start(), calls=%async_computation.29 | async-start | bytes 1179648 | tf_op jit(solution)/shard_map/reduce_scatter | solution.py:139
  505.0 487.6 %reduce-scatter.44.cloned.1.call-start = ((), (), s32[]{:S(2)}) async-start(), calls=%async_computation.28 | async-start | bytes 3538944 | tf_op jit(solution)/shard_map/reduce_scatter | solution.py:136
  (11 other events, 19.8 us)
Sparse Core Ops, SparseCore 0:
  54.1 25.7 all-gather.14
  82.3 25.3 all-gather.16
  115.1 44.0 reduce-scatter.35
  161.1 27.1 all-gather.20
  190.4 27.9 all-gather.18
  220.4 27.4 all-gather.24
  249.9 27.6 all-gather.22
  286.6 43.9 reduce-scatter.39
  332.8 43.1 reduce-scatter.37
  379.2 27.2 all-gather.26
  419.7 43.3 reduce-scatter.41
  466.0 33.4 reduce-scatter.65
  502.8 33.3 reduce-scatter.57
  539.1 33.3 reduce-scatter.55
  575.6 33.3 reduce-scatter.63
  611.9 33.3 reduce-scatter.67
  648.4 33.3 reduce-scatter.59
  684.6 33.3 reduce-scatter.61
  721.3 33.3 reduce-scatter.51
  757.6 33.3 reduce-scatter.53
  795.3 51.3 reduce-scatter.47
  850.6 51.2 reduce-scatter.49
  906.0 36.0 reduce-scatter.45
  946.3 46.2 reduce-scatter.43
where the time goes:
time: 1000 us; the launch traced here: 999 us
  waiting for transfers between devices  759 us (76%)
  blocking collectives  119 us (12%)
  matrix products  45.5 us (5%)
  local copies, waits for them, and re-layouts  41.7 us (4%)
  other arithmetic  16.8 us (2%)
  between operations  16.2 us (2%)
    unnamed x33, waiting for transfers between devices  272 us
    reduce_scatter x1, waiting for transfers between devices, spread(): lax.psum_scatter(pieces[11], 'fsdp', scatter_dimension=1, tiled=True)  55.3 us
    reduce_scatter x1, waiting for transfers between devices, spread(): lax.psum_scatter(pieces[9], 'fsdp', scatter_dimension=0, tiled=True)  54.4 us
    reduce_scatter x1, waiting for transfers between devices, spread(): lax.psum_scatter(pieces[2], 'fsdp', scatter_dimension=0, tiled=True)  50.5 us
    reduce_scatter x1, waiting for transfers between devices, forward_pass(): lax.psum_scatter(jnp.dot(act_up, w_down, preferred_element_type=jnp.float...  44.2 us
    reduce_scatter x1, waiting for transfers between devices, spread(): lax.psum_scatter(pieces[5], 'fsdp', scatter_dimension=1, tiled=True)  40.2 us
    reduce_scatter x1, waiting for transfers between devices, backward_pass(): lax.psum_scatter(jnp.dot(grad_qkv_low, qkv_matrix.T, preferred_element_ty...  40 us
    unnamed x85, local copies, waits for them, and re-layouts  34.7 us
  transfers between devices with their start and end apart: 24, of which 23 were waited for; matrix products, arithmetic and copies ran while one was open for 6% of the time, Pallas kernels for 0%

commit v1 on v0

--- a/solution.py
+++ b/solution.py
@@ -201,7 +201,14 @@
     hidden_one = tokens_wide + attn_term + proj_bias.astype(jnp.float32)
     normed_mlp = layer_norm(hidden_one, mlp_gain.astype(jnp.float32), mlp_shift.astype(jnp.float32))
     act_mlp = normed_mlp.astype(jnp.bfloat16)
-    mlp_inputs = lax.all_gather(act_mlp, "shard", axis=0, tiled=True)
+    ring = [act_mlp]
+    for hop in range(3):
+        ring.append(lax.ppermute(ring[-1], "shard", [(dev, (dev + 1) % 4) for dev in range(4)]))
+    mlp_inputs = jnp.roll(
+        jnp.concatenate(ring[::-1], axis=0),
+        (lax.axis_index("shard") + 1) * ring[0].shape[0],
+        axis=0,
+    )
     pre_act = jnp.dot(mlp_inputs, w_up, preferred_element_type=jnp.float32) + up_bias.astype(
         jnp.float32
     )

time: 1000 us -> 970 us (0.970)
  waiting for transfers between devices: 759 us -> 723 us
    all_gather x1 -> x0, waiting for transfers between devices: 30 us -> none  [forward_pass(): mlp_inputs = lax.all_gather(act_mlp, 'shard', axis=0, tiled=True)]
    ppermute x0 -> x3, waiting for transfers between devices: none -> 18 us  [forward_pass(): lax.ppermute(ring[-1], 'shard', [(dev, (dev + 1) % 4) for dev in range(4)])]
    all_gather x1, waiting for transfers between devices: 15.5 us -> 0.01 us  [collect(): lax.all_gather(params[9], 'fsdp', axis=0, tiled=True)]
    unnamed x85 -> x87, local copies, waits for them, and re-layouts: 34.7 us -> 38.5 us
    unnamed x33 -> x32, waiting for transfers between devices: 272 us -> 272 us
  transfers between devices with their start and end apart: 24 -> 26, of which waited for: 23 -> 23; matrix products, arithmetic and copies ran while one was open for 6% -> 6% of each run, Pallas kernels for 0% -> 0%
where the time goes in v1:
time: 970 us; the launch traced here: 968 us
  waiting for transfers between devices  723 us (75%)
  blocking collectives  120 us (12%)
  local copies, waits for them, and re-layouts  45.5 us (5%)
  matrix products  45 us (5%)
  other arithmetic  17.8 us (2%)
  between operations  15.9 us (2%)
    unnamed x32, waiting for transfers between devices  272 us
    reduce_scatter x1, waiting for transfers between devices, spread(): lax.psum_scatter(pieces[11], 'fsdp', scatter_dimension=1, tiled=True)  55.3 us
    reduce_scatter x1, waiting for transfers between devices, spread(): lax.psum_scatter(pieces[9], 'fsdp', scatter_dimension=0, tiled=True)  54.2 us
    reduce_scatter x1, waiting for transfers between devices, spread(): lax.psum_scatter(pieces[2], 'fsdp', scatter_dimension=0, tiled=True)  50.6 us
    reduce_scatter x1, waiting for transfers between devices, forward_pass(): lax.psum_scatter(jnp.dot(act_up, w_down, preferred_element_type=jnp.float...  44.2 us
    reduce_scatter x1, waiting for transfers between devices, spread(): lax.psum_scatter(pieces[5], 'fsdp', scatter_dimension=1, tiled=True)  40.1 us
    reduce_scatter x1, waiting for transfers between devices, backward_pass(): lax.psum_scatter(jnp.dot(grad_qkv_low, qkv_matrix.T, preferred_element_ty...  39.8 us
    unnamed x87, local copies, waits for them, and re-layouts  38.5 us
  transfers between devices with their start and end apart: 26, of which 23 were waited for; matrix products, arithmetic and copies ran while one was open for 6% of the time, Pallas kernels for 0%

profile of v1, /device:TPU:0, one launch (start us, length us, event | category | flops | bytes accessed | tf_op | source)
XLA Modules:
  0.0 968.3 jit_solution(10072573433023956776)
XLA Ops:
  15.9 15.1 %all-reduce.15 = (bf16[256]{0:T(256)(128)(2,1)S(1)}, bf16[256]{0:T(256)(128)(2,1)S(1)}, bf16[256]{0:T(256)(128)(2,1)S(1)}, bf16[256]{0:T(256)(128)(2,1)S(1)}, bf...) all-reduce(bf16[256]{0:T(256)(128)(2,1)S(1)} %dynamic-update-slice., ...), channel_id=1, replica_groups=mesh['fsdp'=8,'shard'=4] {'fsdp'}, use_global_device_ids=true, to_apply=%add.1 | all-reduce | flops 2048 | bytes 8192
  31.1 11.2 %all-gather.1 = bf16[4,1,256]{2,1,0:T(2,128)(2,1)S(1)} all-gather(bf16[1,1,256]{2,1,0:T(2,128)(2,1)S(1)} %reshape.315), channel_id=1, replica_groups=mesh['fsdp'=8,'shard'=4] {'shard'}, dimensions={0}, use_global_device_ids=true | all-gather | bytes 2560 | tf_op jit(solution)/shard_map/all_gather | solution.py:58
  55.9 9.7 %all-gather.2 = s32[4,1,128]{2,1,0:T(1,128)S(1)} all-gather(s32[1,1,128]{2,1,0:T(1,128)} %bitcast.156), channel_id=1, replica_groups=mesh['fsdp'=8,'shard'=4] {'shard'}, dimensions={0}, use_global_device_ids=true | all-gather | bytes 2560 | tf_op jit(solution)/shard_map/all_gather | solution.py:176
  65.6 9.0 all_gather.86
  79.9 27.8 %all-gather.16.cloned.1.call-done = bf16[1024,3,256]{0,2,1:T(8,128)(2,1)} async-done(((bf16[128,3,256]{0,2,1:T(8,128)(2,1)}), bf16[1024,3,256]{0,2,1:T(8,128)(2,1)}) %all-gather.16.cloned.1.call-update) | async-done | bytes 1572880 | tf_op jit(solution)/shard_map/all_gather | solution.py:44
  117.8 11.1 %all-gather.3 = bf16[4,1,256]{2,1,0:T(2,128)(2,1)S(1)} all-gather(bf16[1,1,256]{2,1,0:T(2,128)(2,1)S(1)} %reshape.319), channel_id=1, replica_groups=mesh['fsdp'=8,'shard'=4] {'shard'}, dimensions={0}, use_global_device_ids=true | all-gather | bytes 2560 | tf_op jit(solution)/shard_map/all_gather | solution.py:59
  128.9 7.6 all-gather.5
  136.5 11.4 %all-gather.4 = bf16[4,1,256]{2,1,0:T(2,128)(2,1)S(1)} all-gather(bf16[1,1,256]{2,1,0:T(2,128)(2,1)S(1)} %reshape.321), channel_id=1, replica_groups=mesh['fsdp'=8,'shard'=4] {'shard'}, dimensions={0}, use_global_device_ids=true | all-gather | bytes 2560 | tf_op jit(solution)/shard_map/all_gather | solution.py:60
  148.0 11.1 %reduce-scatter.36.cloned.1.call-done = f32[128,1024]{1,0:T(8,128)} async-done(((f32[512,1024]{1,0:T(8,128)}), f32[128,1024]{1,0:T(8,128)}) %reduce-scatter.36.cloned.1.call-update) | async-done | bytes 524304 | tf_op jit(solution)/shard_map/reduce_scatter | solution.py:195
  161.2 9.3 collective-permute-done
  170.4 8.7 collective-permute-done.1
  179.2 8.9 all_gather.94
  198.7 19.6 %all-gather.22.cloned.1.call-done = bf16[512,1024]{1,0:T(8,128)(2,1)} async-done(((bf16[128,1024]{1,0:T(8,128)(2,1)}), bf16[512,1024]{1,0:T(8,128)(2,1)}) %all-gather.22.cloned.1.call-update) | async-done | bytes 1048592 | tf_op jit(solution)/shard_map/all_gather | solution.py:263
  218.4 29.6 %all-gather.20.cloned.1.call-done = bf16[1024,1024]{1,0:T(8,128)(2,1)} async-done(((bf16[1024,128]{1,0:T(8,128)(2,1)}), bf16[1024,1024]{1,0:T(8,128)(2,1)}) %all-gather.20.cloned.1.call-update) | async-done | bytes 2097168 | tf_op jit(solution)/shard_map/all_gather | solution.py:53
  262.0 11.1 %all-gather.6 = bf16[4,1,256]{2,1,0:T(2,128)(2,1)S(1)} all-gather(bf16[1,1,256]{2,1,0:T(2,128)(2,1)S(1)} %reshape.325), channel_id=1, replica_groups=mesh['fsdp'=8,'shard'=4] {'shard'}, dimensions={0}, use_global_device_ids=true | all-gather | bytes 2560 | tf_op jit(solution)/shard_map/all_gather | solution.py:62
  273.1 27.7 %reduce-scatter.40.cloned.1.call-done = f32[128,1024]{1,0:T(8,128)} async-done(((f32[512,1024]{1,0:T(8,128)}), f32[128,1024]{1,0:T(8,128)}) %reduce-scatter.40.cloned.1.call-update) | async-done | bytes 524304 | tf_op jit(solution)/shard_map/reduce_scatter | solution.py:272
  302.1 44.2 %reduce-scatter.38.cloned.1.call-done = f32[128,1024]{1,0:T(8,128)} async-done(((f32[512,1024]{1,0:T(8,128)}), f32[128,1024]{1,0:T(8,128)}) %reduce-scatter.38.cloned.1.call-update) | async-done | bytes 524304 | tf_op jit(solution)/shard_map/reduce_scatter | solution.py:216
  349.4 27.4 %all-gather.24.cloned.1.call-done = bf16[512,1024]{1,0:T(8,128)(2,1)} async-done(((bf16[128,1024]{1,0:T(8,128)(2,1)}), bf16[512,1024]{1,0:T(8,128)(2,1)}) %all-gather.24.cloned.1.call-update) | async-done | bytes 1048592 | tf_op jit(solution)/shard_map/all_gather | solution.py:284
  392.4 39.8 %reduce-scatter.42.cloned.1.call-done = f32[128,1024]{1,0:T(8,128)} async-done(((f32[512,1024]{1,0:T(8,128)}), f32[128,1024]{1,0:T(8,128)}) %reduce-scatter.42.cloned.1.call-update) | async-done | bytes 524304 | tf_op jit(solution)/shard_map/reduce_scatter | solution.py:321
  437.3 17.1 %all-reduce.14 = (f32[4,256]{1,0:T(4,128)S(1)}, f32[4,256]{1,0:T(4,128)S(1)}, f32[4,256]{1,0:T(4,128)S(1)}, f32[4,256]{1,0:T(4,128)S(1)}, f32[4,256]{1,0:T(4,128)S(1)}, /*index=5*/f32[4,256]{1,0:T(4,128)S(1)}) all-reduce(f32[4,256]{1,0:T(4,128)S(1)} %reshape.272, ...), channel_id=6, replica_groups=mesh['fsdp'=8,'shard'=4] {'shard'}, use_global_device_ids=true, to_apply=%region_16.17.clone | all-reduce | flops 6144 | bytes 49152
  480.6 24.8 %reduce-scatter.56.cloned.1.call-done = f32[32,1]{1,0:T(8,128)} async-done(((f32[256,1]{1,0:T(8,128)}), f32[32,1]{1,0:T(8,128)}) %reduce-scatter.56.cloned.1.call-update) | async-done | bytes 144
  506.7 35.1 %reduce-scatter.58.cloned.1.call-done = f32[32,1]{1,0:T(8,128)} async-done(((f32[256,1]{1,0:T(8,128)}), f32[32,1]{1,0:T(8,128)}) %reduce-scatter.58.cloned.1.call-update) | async-done | bytes 144
  543.1 35.2 %reduce-scatter.52.cloned.1.call-done = f32[32,1]{1,0:T(8,128)} async-done(((f32[256,1]{1,0:T(8,128)}), f32[32,1]{1,0:T(8,128)}) %reduce-scatter.52.cloned.1.call-update) | async-done | bytes 144
  579.6 34.9 %reduce-scatter.54.cloned.1.call-done = f32[32,1]{1,0:T(8,128)} async-done(((f32[256,1]{1,0:T(8,128)}), f32[32,1]{1,0:T(8,128)}) %reduce-scatter.54.cloned.1.call-update) | async-done | bytes 144
  615.8 35.2 %reduce-scatter.60.cloned.1.call-done = f32[32,1]{1,0:T(8,128)} async-done(((f32[256,1]{1,0:T(8,128)}), f32[32,1]{1,0:T(8,128)}) %reduce-scatter.60.cloned.1.call-update) | async-done | bytes 144
  652.4 34.9 %reduce-scatter.62.cloned.1.call-done = f32[32,1]{1,0:T(8,128)} async-done(((f32[256,1]{1,0:T(8,128)}), f32[32,1]{1,0:T(8,128)}) %reduce-scatter.62.cloned.1.call-update) | async-done | bytes 144
  688.6 35.2 %reduce-scatter.64.cloned.1.call-done = f32[32,1]{1,0:T(8,128)} async-done(((f32[256,1]{1,0:T(8,128)}), f32[32,1]{1,0:T(8,128)}) %reduce-scatter.64.cloned.1.call-update) | async-done | bytes 144
  725.1 35.1 %reduce-scatter.68.cloned.1.call-done = f32[32,1]{1,0:T(8,128)} async-done(((f32[256,1]{1,0:T(8,128)}), f32[32,1]{1,0:T(8,128)}) %reduce-scatter.68.cloned.1.call-update) | async-done | bytes 144
  761.5 54.2 %reduce-scatter.48.cloned.1.call-done = f32[128,1024]{1,0:T(8,128)} async-done(((f32[1024,1024]{1,0:T(8,128)}), f32[128,1024]{1,0:T(8,128)}) %reduce-scatter.48.cloned.1.call-update) | async-done | bytes 524304 | tf_op jit(solution)/shard_map/reduce_scatter | solution.py:143
  815.8 55.3 %reduce-scatter.50.cloned.1.call-done = f32[1024,128]{1,0:T(8,128)} async-done(((f32[1024,1024]{1,0:T(8,128)}), f32[1024,128]{1,0:T(8,128)}) %reduce-scatter.50.cloned.1.call-update) | async-done | bytes 524304 | tf_op jit(solution)/shard_map/reduce_scatter | solution.py:145
  871.0 40.1 %reduce-scatter.46.cloned.1.call-done = f32[256,128]{1,0:T(8,128)} async-done(((f32[256,1024]{1,0:T(8,128)}), f32[256,128]{1,0:T(8,128)}) %reduce-scatter.46.cloned.1.call-update) | async-done | bytes 131088 | tf_op jit(solution)/shard_map/reduce_scatter | solution.py:139
  911.2 50.6 %reduce-scatter.44.cloned.1.call-done = f32[128,3,256]{2,0,1:T(8,128)} async-done(((f32[1024,3,256]{2,0,1:T(8,128)}), f32[128,3,256]{2,0,1:T(8,128)}) %reduce-scatter.44.cloned.1.call-update) | async-done | bytes 393232 | tf_op jit(solution)/shard_map/reduce_scatter | solution.py:136
  (218 shorter events, 124.1 us)
Async XLA Ops:
  7.2 58.4 %copy-start.8 = (bf16[256,128]{1,0:T(8,128)(2,1)S(1)}, bf16[256,128]{1,0:T(8,128)(2,1)}, u32[]{:S(2)}) copy-start(bf16[256,128]{1,0:T(8,128)(2,1)} %param.26) | copy-start | bytes 196612
  7.2 72.7 %all-gather.14.cloned.1.call-start = ((), (), s32[]{:S(2)}) async-start(), calls=%async_computation.17 | async-start | bytes 1310720 | tf_op jit(solution)/shard_map/all_gather | solution.py:175
  54.0 53.7 %all-gather.16.cloned.1.call-start = ((), (), s32[]{:S(2)}) async-start(), calls=%async_computation.18 | async-start | bytes 1769472 | tf_op jit(solution)/shard_map/all_gather | solution.py:44
  55.8 103.3 %reduce-scatter.36.cloned.1.call-start = ((), (), s32[]{:S(2)}) async-start(), calls=%async_computation.19 | async-start | bytes 2621440 | tf_op jit(solution)/shard_map/reduce_scatter | solution.py:195
  74.6 38.6 %copy-start.3 = (bf16[256,1024]{1,0:T(8,128)(2,1)}, bf16[256,1024]{1,0:T(8,128)(2,1)S(1)}, u32[]{:S(2)}) copy-start(bf16[256,1024]{1,0:T(8,128)(2,1)S(1)} %all_gather.86) | copy-start | bytes 1572868
  115.0 44.1 %copy-start = (bf16[128,1024]{1,0:T(8,128)(2,1)S(1)}, bf16[128,1024]{1,0:T(8,128)(2,1)}, u32[]{:S(2)}) copy-start(bf16[128,1024]{1,0:T(8,128)(2,1)} %param.17) | copy-start | bytes 786436
  115.0 64.1 %copy-start.9 = (bf16[1,128]{1,0:T(2,128)(2,1)S(1)}, bf16[1,128]{1,0:T(2,128)(2,1)}, u32[]{:S(2)}) copy-start(bf16[1,128]{1,0:T(2,128)(2,1)} %param.31) | copy-start | bytes 772
  115.1 79.2 %all-gather.18.cloned.1.call-start = ((), (), s32[]{:S(2)}) async-start(), calls=%async_computation.20 | async-start | bytes 2359296 | tf_op jit(solution)/shard_map/all_gather | solution.py:51
  115.6 102.7 %all-gather.22.cloned.1.call-start = ((), (), s32[]{:S(2)}) async-start(), calls=%async_computation.23 | async-start | bytes 1310720 | tf_op jit(solution)/shard_map/all_gather | solution.py:263
  117.2 130.8 %all-gather.20.cloned.1.call-start = ((), (), s32[]{:S(2)}) async-start(), calls=%async_computation.21 | async-start | bytes 2359296 | tf_op jit(solution)/shard_map/all_gather | solution.py:53
  117.8 183.1 %reduce-scatter.40.cloned.1.call-start = ((), (), s32[]{:S(2)}) async-start(), calls=%async_computation.24 | async-start | bytes 2621440 | tf_op jit(solution)/shard_map/reduce_scatter | solution.py:272
  160.7 9.7 %collective-permute-start = (bf16[128,1024]{1,0:T(8,128)(2,1)S(1)}, bf16[128,1024]{1,0:T(8,128)(2,1)S(1)}, u32[]{:S(2)}, u32[]{:S(2)}) collective-permute-start(bf16[128,1024]{1,0:T(8,128)(2,1)S(1)} %add_convert_fusion.1), channel_id=1, source_target_pairs={{0,1},{1,2},{2,3},{3,0},{4,5},{5,6},{6,7},{7,4},{8,9},{9,10},{10,1... | collective-permute-start | bytes 786440 | tf_op jit(solution)/shard_map/ppermute | solution.py:206
  170.4 8.7 collective-permute-start.1
  179.2 8.9 collective-permute-start.2
  248.0 6.2 copy-start.10
  256.7 89.6 %reduce-scatter.38.cloned.1.call-start = ((), (), s32[]{:S(2)}) async-start(), calls=%async_computation.22 | async-start | bytes 2621440 | tf_op jit(solution)/shard_map/reduce_scatter | solution.py:216
  261.9 114.9 %all-gather.24.cloned.1.call-start = ((), (), s32[]{:S(2)}) async-start(), calls=%async_computation.25 | async-start | bytes 1310720 | tf_op jit(solution)/shard_map/all_gather | solution.py:284
  349.3 82.9 %reduce-scatter.42.cloned.1.call-start = ((), (), s32[]{:S(2)}) async-start(), calls=%async_computation.26 | async-start | bytes 2621440 | tf_op jit(solution)/shard_map/reduce_scatter | solution.py:321
  388.7 90.4 %reduce-scatter.66.cloned.1.call-start = ((), (), s32[]{:S(2)}) async-start(), calls=%async_computation.38 | async-start | bytes 589824
  389.8 115.5 %reduce-scatter.56.cloned.1.call-start = ((), (), s32[]{:S(2)}) async-start(), calls=%async_computation.33 | async-start | bytes 147456
  390.7 151.1 %reduce-scatter.58.cloned.1.call-start = ((), (), s32[]{:S(2)}) async-start(), calls=%async_computation.34 | async-start | bytes 147456
  392.2 186.1 %reduce-scatter.52.cloned.1.call-start = ((), (), s32[]{:S(2)}) async-start(), calls=%async_computation.31 | async-start | bytes 147456
  434.9 26.6 %copy-start.15 = (bf16[512,1024]{1,0:T(8,128)(2,1)S(1)}, bf16[512,1024]{1,0:T(8,128)(2,1)}, u32[]{:S(2)}) copy-start(bf16[512,1024]{1,0:T(8,128)(2,1)} %copy-done.14) | copy-start | bytes 3145732
  455.8 158.8 %reduce-scatter.54.cloned.1.call-start = ((), (), s32[]{:S(2)}) async-start(), calls=%async_computation.32 | async-start | bytes 147456
  456.6 194.4 %reduce-scatter.60.cloned.1.call-start = ((), (), s32[]{:S(2)}) async-start(), calls=%async_computation.35 | async-start | bytes 147456
  458.2 229.1 %reduce-scatter.62.cloned.1.call-start = ((), (), s32[]{:S(2)}) async-start(), calls=%async_computation.36 | async-start | bytes 147456
  459.0 264.8 %reduce-scatter.64.cloned.1.call-start = ((), (), s32[]{:S(2)}) async-start(), calls=%async_computation.37 | async-start | bytes 147456
  460.6 299.6 %reduce-scatter.68.cloned.1.call-start = ((), (), s32[]{:S(2)}) async-start(), calls=%async_computation.39 | async-start | bytes 147456
  461.5 354.3 %reduce-scatter.48.cloned.1.call-start = ((), (), s32[]{:S(2)}) async-start(), calls=%async_computation.29 | async-start | bytes 4718592 | tf_op jit(solution)/shard_map/reduce_scatter | solution.py:143
  466.0 405.0 %reduce-scatter.50.cloned.1.call-start = ((), (), s32[]{:S(2)}) async-start(), calls=%async_computation.30 | async-start | bytes 4718592 | tf_op jit(solution)/shard_map/reduce_scatter | solution.py:145
  471.5 439.7 %reduce-scatter.46.cloned.1.call-start = ((), (), s32[]{:S(2)}) async-start(), calls=%async_computation.28 | async-start | bytes 1179648 | tf_op jit(solution)/shard_map/reduce_scatter | solution.py:139
  474.1 487.6 %reduce-scatter.44.cloned.1.call-start = ((), (), s32[]{:S(2)}) async-start(), calls=%async_computation.27 | async-start | bytes 3538944 | tf_op jit(solution)/shard_map/reduce_scatter | solution.py:136
  (11 other events, 19.9 us)
Sparse Core Ops, SparseCore 0:
  54.1 25.7 all-gather.13
  82.3 25.3 all-gather.15
  115.2 43.9 reduce-scatter.35
  161.0 27.2 all-gather.17
  190.4 27.9 all-gather.21
  220.3 27.6 all-gather.19
  256.9 43.9 reduce-scatter.39
  303.1 43.1 reduce-scatter.37
  349.5 27.2 all-gather.23
  388.9 43.3 reduce-scatter.41
  435.4 33.4 reduce-scatter.65
  472.0 33.3 reduce-scatter.55
  508.4 33.3 reduce-scatter.57
  544.9 33.3 reduce-scatter.51
  581.1 33.3 reduce-scatter.53
  617.7 33.3 reduce-scatter.59
  653.9 33.3 reduce-scatter.61
  690.4 33.3 reduce-scatter.63
  726.8 33.3 reduce-scatter.67
  764.4 51.3 reduce-scatter.47
  819.7 51.2 reduce-scatter.49
  875.1 36.0 reduce-scatter.45
  915.5 46.2 reduce-scatter.43
